TPU v7x, 32 devices: a whole 2x2x4 slice. The times are simulated.
32 devices in a mesh: span: 8 (over z, y), plane: 4 (over x, core).
Axes of the slice: x: 2, y: 2, z: 4, core: 2. Of those that a mesh axis runs over, the one named last changes fastest.
Arguments:
- adjoint: float32 [3, 32, 81, 512], P(None, 'span', None, 'plane'), may hold values from -6 to 6
- checkpoints: bfloat16 [8, 2, 32, 81, 512], P(None, None, 'span', None, 'plane'), may hold values from -4 to 4
- checkpoint_step: int32 [3], replicated, may hold values from 0 to 7
- metric: float32 [2, 512], P(None, 'plane'), may hold values from 0.004 to 0.016
- helmholtz_inverse: float32 [32, 81, 81], P('span'), may hold values from -0.08 to 0.8
- wall_element: int32 [1024, 2], replicated, may hold values from 0 to 511
- wall_local: int32 [1024, 2], replicated, may hold values from 0 to 80
- wall_weight: float32 [32, 1024], P('span'), may hold values from 0.7 to 140
Outputs:
- adjoint_next: float32 [3, 32, 81, 512], P(None, 'span', None, 'plane')
- control_gradient: float32 [32, 1024], P('span', 'plane')
All inputs are finite; a program needn't handle non-finite values.
Results may differ from a plain program's by a relative error of at most 0.00065.
Values may be sent and summed in bfloat16 or wider, within the bound.
A program may use at most 128 MiB of HBM per device.

v0:
```python
import jax
import jax.numpy as jnp
import numpy as np
from jax import lax
from jax.sharding import PartitionSpec as P

P_SIZE = 8
NSTEP = 3
HIGHEST = lax.Precision.HIGHEST


def chebyshev_matrix(degree):
    points = np.arange(degree + 1)
    abscissa = np.cos(np.pi * points / degree)
    signed = np.where((points == 0) | (points == degree), 2.0, 1.0) * (-1.0) ** points
    spacing = abscissa[:, None] - abscissa[None, :] + np.eye(degree + 1)
    matrix = signed[:, None] / signed[None, :] / spacing
    return matrix - np.eye(degree + 1) * np.sum(matrix, axis=1)[:, None]


def fourier_table(length):
    row_index = np.arange(length)[:, None]
    column = np.arange(length)[None, :]
    wavenumber = (row_index + 1) // 2
    phase_angle = 2.0 * np.pi * wavenumber * column / length
    parity = row_index % 2
    base_rows = np.where(
        row_index == 0, 1.0, np.where(parity == 1, np.cos(phase_angle), np.sin(phase_angle))
    )
    row_scale = np.where(
        (row_index == 0) | (row_index == length - 1), 1.0 / np.sqrt(length), np.sqrt(2.0 / length)
    )
    return base_rows * row_scale


def transport(field_data, velocity, metric):
    side_nodes = P_SIZE + 1
    matrix = jnp.asarray(chebyshev_matrix(P_SIZE), jnp.float32)
    shaped = field_data.reshape(
        field_data.shape[0], field_data.shape[1], side_nodes, side_nodes, field_data.shape[3]
    )
    first_dir = jnp.einsum("ai,czibe->czabe", matrix, shaped, precision=HIGHEST).reshape(
        field_data.shape
    )
    second_dir = jnp.einsum("bi,czaie->czabe", matrix, shaped, precision=HIGHEST).reshape(
        field_data.shape
    )
    speed_data = velocity.astype(jnp.float32)
    return (
        field_data
        + speed_data[0] * (metric[0] * first_dir)
        + speed_data[1] * (metric[1] * second_dir)
    )


def forward_modes(gathered):
    basis_table = jnp.asarray(fourier_table(gathered.shape[1]), jnp.float32)
    return jnp.einsum("jz,czqe->cjqe", basis_table, gathered, precision=HIGHEST)


def backward_planes(solved):
    basis_table = jnp.asarray(fourier_table(solved.shape[1]), jnp.float32)
    return jnp.einsum("jz,cjqe->czqe", basis_table, solved, precision=HIGHEST)


def solve_modes(inverse_block, coefficients):
    return jnp.einsum("jqr,cjre->cjqe", inverse_block, coefficients, precision=HIGHEST)


def to_plane_layout(point_data):
    return lax.all_to_all(point_data, "span", split_axis=1, concat_axis=3, tiled=True)


def wall_terms(field_one, speed_one, flat_index, inside, wall_count):
    rows = field_one.shape[0]
    values = jnp.take(field_one.reshape(rows, -1), flat_index, axis=1)
    speeds = jnp.take(speed_one.reshape(rows, -1), flat_index, axis=1).astype(jnp.float32)
    product = jnp.where(inside, values * speeds, 0.0).reshape(rows, wall_count, 2)
    return jnp.sum(product, axis=2)


def on_device(
    adjoint,
    checkpoints,
    checkpoint_step,
    metric,
    helmholtz_inverse,
    wall_element,
    wall_local,
    wall_weight,
):
    planes_dev = adjoint.shape[1]
    elems_dev = adjoint.shape[3]
    wall_count = wall_element.shape[0]
    span_count = lax.axis_size("span")
    all_modes = lax.all_gather(helmholtz_inverse, "span", axis=0, tiled=True)
    offset = lax.axis_index("plane") * elems_dev
    local_element = wall_element - offset
    inside = ((local_element >= 0) & (local_element < elems_dev)).reshape(-1)
    flat_index = (wall_local * elems_dev + jnp.clip(local_element, 0, elems_dev - 1)).reshape(-1)
    partial_sum = jnp.zeros((planes_dev, wall_count), jnp.float32)
    for substep in range(NSTEP):
        velocity = lax.dynamic_index_in_dim(
            checkpoints, checkpoint_step[substep], 0, keepdims=False
        )
        advected = transport(adjoint, velocity, metric)
        point_data = backward_planes(
            solve_modes(
                all_modes,
                forward_modes(
                    lax.all_to_all(advected, "span", split_axis=3, concat_axis=1, tiled=True)
                ),
            )
        )
        adjoint = to_plane_layout(point_data)
        partial_sum = partial_sum + wall_terms(
            adjoint[1], velocity[1], flat_index, inside, wall_count
        )
    weighted = wall_weight * partial_sum
    grad_share = lax.psum_scatter(weighted, "plane", scatter_dimension=1, tiled=True)
    square_total = lax.psum(jnp.sum(grad_share * grad_share), ("span", "plane"))
    inverse_rms = lax.rsqrt(square_total / (planes_dev * span_count * wall_count) + 1e-06)
    return (adjoint, grad_share * inverse_rms)


def solution(mesh):
    placed = (
        P(None, "span", None, "plane"),
        P(None, None, "span", None, "plane"),
        P(),
        P(None, "plane"),
        P("span", None, None),
        P(),
        P(),
        P("span", None),
    )
    return jax.shard_map(
        on_device,
        mesh=mesh,
        in_specs=placed,
        out_specs=(P(None, "span", None, "plane"), P("span", "plane")),
        check_vma=False,
    )
```

profile of v0, /device:TPU:0, one launch (start us, length us, event | category | flops | bytes accessed | tf_op | source)
XLA Modules:
  0.0 388.5 jit_solution(4690724075645304346)
XLA Ops:
  20.4 7.3 %all-to-all-start = ((f32[3,4,81,128]{2,1,0,3:T(4,128)}), f32[3,4,81,128]{2,1,0,3:T(4,128)S(1)}, u32[]{:S(2)}, u32[]{:S(2)}) async-start(f32[3,4,81,128]{2,1,0,3:T(4,128)} %copy.127), calls=%async_computation | async-start | bytes 1572864 | tf_op jit(solution)/shard_map/all_to_all | solution.py:111
  27.8 47.5 %all_gather.3 = f32[32,81,81]{2,1,0:T(8,128)S(1)} all-gather(f32[4,81,81]{2,1,0:T(8,128)S(1)} %copy.131), channel_id=1, replica_groups=mesh['span'=8,'plane'=4] {'span'}, dimensions={0}, use_global_device_ids=true | all-gather | bytes 944784 | tf_op jit(solution)/shard_map/all_gather | solution.py:96
  77.0 2.7 fusion.6
  82.1 4.0 %all-to-all-start.1 = ((f32[3,32,81,16]{2,3,0,1:T(8,128)}), f32[3,32,81,16]{2,3,0,1:T(8,128)S(1)}, u32[]{:S(2)}, u32[]{:S(2)}) async-start(f32[3,32,81,16]{2,3,0,1:T(8,128)} %copy.135), calls=%async_computation.1 | async-start | bytes 1572864 | tf_op jit(solution)/shard_map/all_to_all | solution.py:71
  86.9 15.1 %all-to-all-done.1 = f32[3,32,81,16]{2,3,0,1:T(8,128)S(1)} async-done(((f32[3,32,81,16]{2,3,0,1:T(8,128)}), f32[3,32,81,16]{2,3,0,1:T(8,128)S(1)}, u32[]{:S(2)}, u32[]{:S(2)}) %all-to-all-start.1) | async-done | bytes 497696 | tf_op jit(solution)/shard_map/all_to_all | solution.py:71
  102.0 3.0 copy.136
  105.0 3.2 reshape.90
  116.9 21.5 %all_to_all.108 = f32[3,4,81,128]{2,1,0,3:T(4,128)S(1)} all-to-all(f32[3,4,81,128]{2,1,0,3:T(4,128)S(1)} %copy.143), channel_id=1, replica_groups=mesh['span'=8,'plane'=4] {'span'}, dimensions={3} | all-to-all | bytes 995328 | tf_op jit(solution)/shard_map/all_to_all | solution.py:111
  140.2 2.7 fusion.9
  144.4 22.6 %all_to_all.109 = f32[3,32,81,16]{2,3,0,1:T(8,128)S(1)} all-to-all(f32[3,32,81,16]{2,3,0,1:T(8,128)S(1)} %copy.150), channel_id=1, replica_groups=mesh['span'=8,'plane'=4] {'span'}, dimensions={1} | all-to-all | bytes 995328 | tf_op jit(solution)/shard_map/all_to_all | solution.py:71
  167.0 3.1 copy.151
  170.1 3.2 reshape.93
  182.7 3.6 all-to-all-start.4
  186.3 19.8 %all-to-all-done.4 = f32[3,4,81,128]{2,1,0,3:T(4,128)S(1)} async-done(((f32[3,4,81,128]{2,1,0,3:T(4,128)}), f32[3,4,81,128]{2,1,0,3:T(4,128)S(1)}, u32[]{:S(2)}, u32[]{:S(2)}) %all-to-all-start.4) | async-done | bytes 497696 | tf_op jit(solution)/shard_map/all_to_all | solution.py:111
  207.4 2.7 fusion.12
  212.5 3.5 all-to-all-start.5
  218.4 2.6 copy.172
  223.3 7.7 %gather_fusion.3 = bf16[2048,4]{1,0:T(8,128)(2,1)S(1)} fusion(bf16[4,10368]{0,1:T(8,128)(2,1)} %bitcast.184, s32[2048]{0:T(1024)S(1)} %fusion.33), kind=kCustom, calls=%fused_computation.4.clone | custom fusion | bytes 40960 | tf_op jit(solution)/shard_map/jit(_take)/gather | solution.py:77
  231.0 9.7 %gather_fusion.5 = bf16[2048,4]{1,0:T(8,128)(2,1)} fusion(bf16[4,10368]{0,1:T(8,128)(2,1)} %bitcast.185, s32[2048]{0:T(1024)S(1)} %fusion.33), kind=kCustom, calls=%fused_computation.5.clone | custom fusion | bytes 40960 | tf_op jit(solution)/shard_map/jit(_take)/gather | solution.py:77
  240.7 2.4 copy.170
  243.1 9.8 %gather_fusion.1 = bf16[2048,4]{1,0:T(8,128)(2,1)} fusion(bf16[4,10368]{0,1:T(8,128)(2,1)} %bitcast.186, s32[2048]{0:T(1024)S(1)} %fusion.33), kind=kCustom, calls=%fused_computation.1.clone | custom fusion | bytes 40960 | tf_op jit(solution)/shard_map/jit(_take)/gather | solution.py:77
  254.3 5.3 %copy.169 = f32[1,4,81,8,16]{1,4,3,2,0:T(8,128)} copy(f32[1,4,81,8,16]{4,3,1,2,0:T(8,128)S(1)} %slice.102) | data formatting | bytes 331776 | tf_op jit(solution)/shard_map/slice | solution.py:117
  259.6 10.1 %gather_fusion = f32[2048,4]{1,0:T(8,128)} fusion(f32[4,10368]{0,1:T(8,128)} %bitcast.167, s32[2048]{0:T(1024)S(1)} %fusion.33), kind=kCustom, calls=%fused_computation.clone | custom fusion | bytes 73728 | tf_op jit(solution)/shard_map/jit(_take)/gather | solution.py:76
  271.1 5.3 %copy.171 = f32[1,4,81,8,16]{1,4,3,2,0:T(8,128)} copy(f32[1,4,81,8,16]{4,3,1,2,0:T(8,128)S(1)} %slice.103) | data formatting | bytes 331776 | tf_op jit(solution)/shard_map/slice | solution.py:117
  276.4 10.1 %gather_fusion.2 = f32[2048,4]{1,0:T(8,128)} fusion(f32[4,10368]{0,1:T(8,128)} %bitcast.168, s32[2048]{0:T(1024)S(1)} %fusion.33), kind=kCustom, calls=%fused_computation.2.clone | custom fusion | bytes 73728 | tf_op jit(solution)/shard_map/jit(_take)/gather | solution.py:76
  286.6 5.7 %copy.173 = f32[1,4,81,8,16]{1,4,3,2,0:T(8,128)} copy(f32[1,4,81,8,16]{2,4,3,1,0:T(8,128)S(1)} %slice.104) | data formatting | bytes 331776 | tf_op jit(solution)/shard_map/slice | solution.py:117
  292.3 10.1 %gather_fusion.4 = f32[2048,4]{1,0:T(8,128)} fusion(f32[4,10368]{0,1:T(8,128)} %bitcast.169, s32[2048]{0:T(1024)S(1)} %fusion.33), kind=kCustom, calls=%fused_computation.3.clone | custom fusion | bytes 73728 | tf_op jit(solution)/shard_map/jit(_take)/gather | solution.py:76
  302.3 4.6 %fusion.16 = (f32[4,2048]{0,1:T(8,128)}, f32[4,2048]{0,1:T(8,128)S(1)}, f32[4,2048]{0,1:T(8,128)S(1)}) fusion(f32[2048,4]{1,0:T(8,128)} %gather_fusion.2, bf16[2048,4]{1,0:T(8,128)(2,1)S(1)} %gather_fusion.3, pred[2048]{0:T(1024)(128)(4,1)S(1)} %compare_and_fusion.1, pred[2048]{0:T(1024)(128)(4,1)S(1)} %reshape.96, bf16[2048,4]{1,0:T(8,128)(2,1)} %gather_fusion.5, ...), kind=kLoop, calls=%fused_computation.30 | loop fusion | flops 122880 | bytes 249856 | tf_op jit(solution)/shard_map/jit(_where)/select_n | solution.py:78
  306.9 2.5 reduce_sum.37
  309.5 2.3 reduce_sum.38
  314.9 23.1 %reduce-scatter.4.cloned.1.call-done = f32[256,4]{1,0:T(8,128)} async-done(((f32[1024,4]{1,0:T(8,128)}), f32[256,4]{1,0:T(8,128)}) %reduce-scatter.4.cloned.1.call-update) | async-done | bytes 4112
  340.6 39.5 %psum.7 = f32[]{:T(128)} all-reduce(f32[]{:T(128)} %multiply_reduce_fusion), channel_id=1, replica_groups=mesh['span'=8,'plane'=4] {'span','plane'}, use_global_device_ids=true, to_apply=%region_5.8 | all-reduce | flops 1 | bytes 8 | tf_op jit(solution)/shard_map/psum | solution.py:121
  (120 shorter events, 51.0 us)
Async XLA Ops:
  7.2 7.4 %copy-start.13 = (f32[9,9,1,1,1]{1,0,4,3,2:T(8,128)S(1)}, f32[9,9,1,1,1]{1,0,4,3,2:T(8,128)}, u32[]{:S(2)}) copy-start(f32[9,9,1,1,1]{1,0,4,3,2:T(8,128)} %constant.58) | copy-start | bytes 976
  7.2 7.4 %copy-start = (f32[3,4,81,128]{3,1,2,0:T(4,128)S(1)}, f32[3,4,81,128]{3,1,2,0:T(4,128)}, u32[]{:S(2)}) copy-start(f32[3,4,81,128]{3,1,2,0:T(4,128)} %param.21) | copy-start | bytes 1492996
  12.6 2.8 copy-start.24
  15.4 3.6 copy-start.18
  15.4 3.6 copy-start.21
  19.3 8.5 %copy-start.14 = (f32[4,81,81]{2,0,1:T(4,128)S(1)}, f32[4,81,81]{2,0,1:T(4,128)}, u32[]{:S(2)}) copy-start(f32[4,81,81]{2,0,1:T(4,128)} %param.25) | copy-start | bytes 314932
  20.4 54.8 %all-to-all-start = ((f32[3,4,81,128]{2,1,0,3:T(4,128)}), f32[3,4,81,128]{2,1,0,3:T(4,128)S(1)}, u32[]{:S(2)}, u32[]{:S(2)}) async-start(f32[3,4,81,128]{2,1,0,3:T(4,128)} %copy.127), calls=%async_computation | async-start | bytes 1572864 | tf_op jit(solution)/shard_map/all_to_all | solution.py:111
  75.2 0.7 copy-start.10
  82.1 19.9 %all-to-all-start.1 = ((f32[3,32,81,16]{2,3,0,1:T(8,128)}), f32[3,32,81,16]{2,3,0,1:T(8,128)S(1)}, u32[]{:S(2)}, u32[]{:S(2)}) async-start(f32[3,32,81,16]{2,3,0,1:T(8,128)} %copy.135), calls=%async_computation.1 | async-start | bytes 1572864 | tf_op jit(solution)/shard_map/all_to_all | solution.py:71
  111.8 3.3 copy-start.4
  112.8 2.5 copy-start.2
  115.1 1.0 copy-start.7
  115.1 1.1 copy-start.8
  115.1 1.1 copy-start.9
  115.1 1.1 copy-start.19
  115.1 1.1 copy-start.22
  138.4 0.7 copy-start.11
  176.9 3.3 copy-start.3
  177.9 2.5 copy-start.1
  180.2 1.0 copy-start.6
  180.2 1.0 copy-start.20
  180.2 1.0 copy-start.23
  182.7 23.4 %all-to-all-start.4 = ((f32[3,4,81,128]{2,1,0,3:T(4,128)}), f32[3,4,81,128]{2,1,0,3:T(4,128)S(1)}, u32[]{:S(2)}, u32[]{:S(2)}) async-start(f32[3,4,81,128]{2,1,0,3:T(4,128)} %copy.158), calls=%async_computation.4 | async-start | bytes 1572864 | tf_op jit(solution)/shard_map/all_to_all | solution.py:111
  186.3 20.0 %copy-start.12 = (f32[32,32,1,1]{1,0,3,2:T(8,128)S(1)}, f32[32,32,1,1]{1,0,3,2:T(8,128)}, u32[]{:S(2)}) copy-start(f32[32,32,1,1]{1,0,3,2:T(8,128)} %constant.59) | copy-start | bytes 12292
  211.1 5.0 %copy-start.15 = (s32[1024,2]{0,1:T(2,128)S(1)}, s32[1024,2]{0,1:T(2,128)}, u32[]{:S(2)}) copy-start(s32[1024,2]{0,1:T(2,128)} %param.26) | copy-start | bytes 24580
  211.1 5.7 %copy-start.17 = (s32[1024,2]{0,1:T(2,128)S(1)}, s32[1024,2]{0,1:T(2,128)}, u32[]{:S(2)}) copy-start(s32[1024,2]{0,1:T(2,128)} %param.27) | copy-start | bytes 24580
  212.5 74.0 %all-to-all-start.5 = ((f32[3,32,81,16]{2,3,0,1:T(8,128)}), f32[3,32,81,16]{2,3,0,1:T(8,128)S(1)}, u32[]{:S(2)}, u32[]{:S(2)}) async-start(f32[3,32,81,16]{2,3,0,1:T(8,128)} %copy.165), calls=%async_computation.5 | async-start | bytes 1572864 | tf_op jit(solution)/shard_map/all_to_all | solution.py:71
  216.0 121.9 %reduce-scatter.4.cloned.1.call-start = ((), (), s32[]{:S(2)}) async-start(), calls=%async_computation.7 | async-start | bytes 655360
  311.8 1.3 copy-start.5
  313.1 0.7 copy-start.16
Sparse Core Ops, SparseCore 0:
  315.0 22.9 reduce-scatter.3
where the time goes:
time: 396 us; the launch traced here: 388 us
  blocking collectives  131 us (33%)
  local copies, waits for them, and re-layouts  121 us (31%)
  waiting for transfers between devices  58 us (15%)
  matrix products  24.4 us (6%)
  between operations  21.5 us (5%)
  starting transfers between devices  18.5 us (5%)
  other arithmetic  13.9 us (4%)
    all_gather x1, blocking collectives, on_device(): all_modes = lax.all_gather(helmholtz_inverse, 'span', axis=0, tiled=True)  47.5 us
    psum x1, blocking collectives, on_device(): square_total = lax.psum(jnp.sum(grad_share * grad_share), ('span', 'plane'))  39.5 us
    gather x3, local copies, waits for them, and re-layouts, wall_terms(): values = jnp.take(field_one.reshape(rows, -1), flat_index, axis=1)  30.2 us
    gather x3, local copies, waits for them, and re-layouts, wall_terms(): jnp.take(speed_one.reshape(rows, -1), flat_index, axis=1)  27.2 us
    unnamed x2, waiting for transfers between devices  23.1 us
    all_to_all x1, blocking collectives, to_plane_layout(): lax.all_to_all(point_data, 'span', split_axis=1, concat_axis=3, tiled=True)  22.6 us
    all_to_all x1, blocking collectives, on_device(): lax.all_to_all(advected, 'span', split_axis=3, concat_axis=1, tiled=True)  21.5 us
    all_to_all x2, waiting for transfers between devices, on_device(): lax.all_to_all(advected, 'span', split_axis=3, concat_axis=1, tiled=True)  19.8 us
  transfers between devices with their start and end apart: 5, of which 3 were waited for; matrix products, arithmetic and copies ran while one was open for 18% of the time, Pallas kernels for 0%

commit v1 on v0

--- a/solution.py
+++ b/solution.py
@@ -7,6 +7,26 @@
 P_SIZE = 8
 NSTEP = 3
 HIGHEST = lax.Precision.HIGHEST
+
+
+def view_shelves_over_axis(xx, dim_i, k_dim):
+    x_next, small = (lax.psum(1, axis_name="span"), lax.axis_index("span"))
+    finding = xx.shape[dim_i] // x_next
+    reached = list(xx.shape)
+    reached[dim_i] = finding
+    q_next = reached[k_dim]
+    reached[k_dim] = q_next * x_next
+    big = jnp.zeros(reached, xx.dtype)
+    rr = 0
+    while rr < x_next:
+        e_now = lax.dynamic_slice_in_dim(xx, (small ^ rr) * finding, finding, axis=dim_i)
+        if rr:
+            e_now = lax.ppermute(
+                e_now, axis_name="span", perm=[(at, at ^ rr) for at in range(x_next)]
+            )
+        big = lax.dynamic_update_slice_in_dim(big, e_now, (small ^ rr) * q_next, axis=k_dim)
+        rr += 1
+    return big
 
 
 def chebyshev_matrix(degree):
@@ -105,12 +125,7 @@
         )
         advected = transport(adjoint, velocity, metric)
         point_data = backward_planes(
-            solve_modes(
-                all_modes,
-                forward_modes(
-                    lax.all_to_all(advected, "span", split_axis=3, concat_axis=1, tiled=True)
-                ),
-            )
+            solve_modes(all_modes, forward_modes(view_shelves_over_axis(advected, 3, k_dim=1)))
         )
         adjoint = to_plane_layout(point_data)
         partial_sum = partial_sum + wall_terms(

time: 396 us -> 626 us (1.58)
  waiting for transfers between devices: 58 us -> 204 us
  local copies, waits for them, and re-layouts: 121 us -> 157 us
  starting transfers between devices: 18.5 us -> 48.3 us
  blocking collectives: 131 us -> 147 us
    ppermute x0 -> x21, waiting for transfers between devices: none -> 154 us  [view_shelves_over_axis(): lax.ppermute(e_now, axis_name='span', perm=[(at, at ^ rr) for at in range...]
    all_gather x1, blocking collectives: 47.5 us -> 107 us  [on_device(): all_modes = lax.all_gather(helmholtz_inverse, 'span', axis=0, tiled=True)]
    all_to_all x2 -> x0, blocking collectives: 44.2 us -> none  [the longest x1 22.6 us: to_plane_layout(): lax.all_to_all(point_data, 'span', split_axis=1, concat_axis=3, tiled=True)]
    ppermute x0 -> x21, starting transfers between devices: none -> 36.8 us  [view_shelves_over_axis(): lax.ppermute(e_now, axis_name='span', perm=[(at, at ^ rr) for at in range...]
    ppermute x0 -> x21, local copies, waits for them, and re-layouts: none -> 25.6 us  [view_shelves_over_axis(): lax.ppermute(e_now, axis_name='span', perm=[(at, at ^ rr) for at in range...]
    all_to_all x2 -> x0, waiting for transfers between devices: 19.8 us -> none  [on_device(): lax.all_to_all(advected, 'span', split_axis=3, concat_axis=1, tiled=True)]
    dynamic_slice x0 -> x6, local copies, waits for them, and re-layouts: none -> 11.7 us  [view_shelves_over_axis(): lax.dynamic_slice_in_dim(xx, (small ^ rr) * finding, finding, axis=dim_i)]
    all_to_all x2 -> x0, starting transfers between devices: 10.9 us -> none  [on_device(): lax.all_to_all(advected, 'span', split_axis=3, concat_axis=1, tiled=True)]
  transfers between devices with their start and end apart: 5 -> 25, of which waited for: 3 -> 11; matrix products, arithmetic and copies ran while one was open for 18% -> 15% of each run, Pallas kernels for 0% -> 0%
where the time goes in v1:
time: 626 us; the launch traced here: 615 us
  waiting for transfers between devices  204 us (33%)
  local copies, waits for them, and re-layouts  157 us (25%)
  blocking collectives  147 us (23%)
  starting transfers between devices  48.3 us (8%)
  matrix products  23.5 us (4%)
  between operations  21.9 us (3%)
  other arithmetic  13.9 us (2%)
    ppermute x21, waiting for transfers between devices, view_shelves_over_axis(): lax.ppermute(e_now, axis_name='span', perm=[(at, at ^ rr) for at in range...  154 us
    all_gather x1, blocking collectives, on_device(): all_modes = lax.all_gather(helmholtz_inverse, 'span', axis=0, tiled=True)  107 us
    psum x1, blocking collectives, on_device(): square_total = lax.psum(jnp.sum(grad_share * grad_share), ('span', 'plane'))  39.5 us
    ppermute x21, starting transfers between devices, view_shelves_over_axis(): lax.ppermute(e_now, axis_name='span', perm=[(at, at ^ rr) for at in range...  36.8 us
    gather x3, local copies, waits for them, and re-layouts, wall_terms(): values = jnp.take(field_one.reshape(rows, -1), flat_index, axis=1)  30.2 us
    gather x3, local copies, waits for them, and re-layouts, wall_terms(): jnp.take(speed_one.reshape(rows, -1), flat_index, axis=1)  27.1 us
    all_to_all x3, waiting for transfers between devices, to_plane_layout(): lax.all_to_all(point_data, 'span', split_axis=1, concat_axis=3, tiled=True)  25.7 us
    ppermute x21, local copies, waits for them, and re-layouts, view_shelves_over_axis(): lax.ppermute(e_now, axis_name='span', perm=[(at, at ^ rr) for at in range...  25.6 us
  transfers between devices with their start and end apart: 25, of which 11 were waited for; matrix products, arithmetic and copies ran while one was open for 15% of the time, Pallas kernels for 0%

profile of v1, /device:TPU:0, one launch (start us, length us, event | category | flops | bytes accessed | tf_op | source)
XLA Modules:
  0.0 615.1 jit_solution(16865341974378185923)
XLA Ops:
  19.2 3.7 constant_dynamic-slice_fusion.19
  22.9 6.0 collective-permute-start.6
  33.6 107.5 %all_gather.3 = f32[32,81,81]{2,1,0:T(8,128)S(1)} all-gather(f32[4,81,81]{2,1,0:T(8,128)S(1)} %copy.75), channel_id=1, replica_groups=mesh['span'=8,'plane'=4] {'span'}, dimensions={0}, use_global_device_ids=true | all-gather | bytes 944784 | tf_op jit(solution)/shard_map/all_gather | solution.py:116
  142.8 10.9 %collective-permute-done.1 = f32[3,4,81,16]{3,1,2,0:T(4,128)} collective-permute-done((f32[3,4,81,16]{3,1,2,0:T(4,128)}, f32[3,4,81,16]{3,1,2,0:T(4,128)}, u32[]{:S(2)}, u32[]{:S(2)}) %collective-permute-start.1) | collective-permute-done | bytes 62240 | tf_op jit(solution)/shard_map/ppermute | solution.py:24
  154.9 8.8 %collective-permute-done.2 = f32[3,4,81,16]{3,1,2,0:T(4,128)} collective-permute-done((f32[3,4,81,16]{3,1,2,0:T(4,128)}, f32[3,4,81,16]{3,1,2,0:T(4,128)}, u32[]{:S(2)}, u32[]{:S(2)}) %collective-permute-start.2) | collective-permute-done | bytes 62240 | tf_op jit(solution)/shard_map/ppermute | solution.py:24
  176.1 3.5 all-to-all-start
  180.4 12.4 %all-to-all-done = f32[3,32,81,16]{2,3,0,1:T(8,128)S(1)} async-done(((f32[3,32,81,16]{2,3,0,1:T(8,128)}), f32[3,32,81,16]{2,3,0,1:T(8,128)S(1)}, u32[]{:S(2)}, u32[]{:S(2)}) %all-to-all-start) | async-done | bytes 497696 | tf_op jit(solution)/shard_map/all_to_all | solution.py:91
  195.8 3.5 reshape.90
  207.6 3.8 constant_dynamic-slice_fusion.11
  220.7 10.5 %collective-permute-done.7 = f32[3,4,81,16]{3,1,2,0:T(4,128)} collective-permute-done((f32[3,4,81,16]{3,1,2,0:T(4,128)}, f32[3,4,81,16]{3,1,2,0:T(4,128)}, u32[]{:S(2)}, u32[]{:S(2)}) %collective-permute-start.7) | collective-permute-done | bytes 62240 | tf_op jit(solution)/shard_map/ppermute | solution.py:24
  232.9 30.7 %collective-permute-done.8 = f32[3,4,81,16]{3,1,2,0:T(4,128)} collective-permute-done((f32[3,4,81,16]{3,1,2,0:T(4,128)}, f32[3,4,81,16]{3,1,2,0:T(4,128)}, u32[]{:S(2)}, u32[]{:S(2)}) %collective-permute-start.8) | collective-permute-done | bytes 62240 | tf_op jit(solution)/shard_map/ppermute | solution.py:24
  267.1 26.8 %collective-permute-done.9 = f32[3,4,81,16]{3,1,2,0:T(4,128)} collective-permute-done((f32[3,4,81,16]{3,1,2,0:T(4,128)}, f32[3,4,81,16]{3,1,2,0:T(4,128)}, u32[]{:S(2)}, u32[]{:S(2)}) %collective-permute-start.9) | collective-permute-done | bytes 62240 | tf_op jit(solution)/shard_map/ppermute | solution.py:24
  306.1 4.4 all-to-all-start.1
  310.5 13.3 %all-to-all-done.1 = f32[3,32,81,16]{2,3,0,1:T(8,128)S(1)} async-done(((f32[3,32,81,16]{2,3,0,1:T(8,128)}), f32[3,32,81,16]{2,3,0,1:T(8,128)S(1)}, u32[]{:S(2)}, u32[]{:S(2)}) %all-to-all-start.1) | async-done | bytes 497696 | tf_op jit(solution)/shard_map/all_to_all | solution.py:91
  338.5 3.5 constant_dynamic-slice_fusion.3
  351.3 10.6 %collective-permute-done.14 = f32[3,4,81,16]{3,1,2,0:T(4,128)} collective-permute-done((f32[3,4,81,16]{3,1,2,0:T(4,128)}, f32[3,4,81,16]{3,1,2,0:T(4,128)}, u32[]{:S(2)}, u32[]{:S(2)}) %collective-permute-start.14) | collective-permute-done | bytes 62240 | tf_op jit(solution)/shard_map/ppermute | solution.py:24
  364.0 29.7 %collective-permute-done.15 = f32[3,4,81,16]{3,1,2,0:T(4,128)} collective-permute-done((f32[3,4,81,16]{3,1,2,0:T(4,128)}, f32[3,4,81,16]{3,1,2,0:T(4,128)}, u32[]{:S(2)}, u32[]{:S(2)}) %collective-permute-start.15) | collective-permute-done | bytes 62240 | tf_op jit(solution)/shard_map/ppermute | solution.py:24
  393.7 4.7 collective-permute-start.16
  399.7 25.9 %collective-permute-done.16 = f32[3,4,81,16]{3,1,2,0:T(4,128)} collective-permute-done((f32[3,4,81,16]{3,1,2,0:T(4,128)}, f32[3,4,81,16]{3,1,2,0:T(4,128)}, u32[]{:S(2)}, u32[]{:S(2)}) %collective-permute-start.16) | collective-permute-done | bytes 62240 | tf_op jit(solution)/shard_map/ppermute | solution.py:24
  437.9 3.6 all-to-all-start.2
  448.8 7.7 %gather_fusion.3 = bf16[2048,4]{1,0:T(8,128)(2,1)S(1)} fusion(bf16[4,10368]{0,1:T(8,128)(2,1)} %bitcast.169, s32[2048]{0:T(1024)S(1)} %fusion.30), kind=kCustom, calls=%fused_computation.4.clone | custom fusion | bytes 40960 | tf_op jit(solution)/shard_map/jit(_take)/gather | solution.py:97
  456.4 9.7 %gather_fusion.5 = bf16[2048,4]{1,0:T(8,128)(2,1)} fusion(bf16[4,10368]{0,1:T(8,128)(2,1)} %bitcast.170, s32[2048]{0:T(1024)S(1)} %fusion.30), kind=kCustom, calls=%fused_computation.5.clone | custom fusion | bytes 40960 | tf_op jit(solution)/shard_map/jit(_take)/gather | solution.py:97
  468.6 9.7 %gather_fusion.1 = bf16[2048,4]{1,0:T(8,128)(2,1)} fusion(bf16[4,10368]{0,1:T(8,128)(2,1)} %bitcast.171, s32[2048]{0:T(1024)S(1)} %fusion.30), kind=kCustom, calls=%fused_computation.1.clone | custom fusion | bytes 40960 | tf_op jit(solution)/shard_map/jit(_take)/gather | solution.py:97
  479.7 5.3 copy.121
  485.0 10.1 %gather_fusion = f32[2048,4]{1,0:T(8,128)} fusion(f32[4,10368]{0,1:T(8,128)} %bitcast.158, s32[2048]{0:T(1024)S(1)} %fusion.30), kind=kCustom, calls=%fused_computation.clone | custom fusion | bytes 73728 | tf_op jit(solution)/shard_map/jit(_take)/gather | solution.py:96
  496.5 5.3 copy.123
  501.8 10.1 %gather_fusion.2 = f32[2048,4]{1,0:T(8,128)} fusion(f32[4,10368]{0,1:T(8,128)} %bitcast.159, s32[2048]{0:T(1024)S(1)} %fusion.30), kind=kCustom, calls=%fused_computation.2.clone | custom fusion | bytes 73728 | tf_op jit(solution)/shard_map/jit(_take)/gather | solution.py:96
  512.0 5.7 copy.125
  517.7 10.1 %gather_fusion.4 = f32[2048,4]{1,0:T(8,128)} fusion(f32[4,10368]{0,1:T(8,128)} %bitcast.160, s32[2048]{0:T(1024)S(1)} %fusion.30), kind=kCustom, calls=%fused_computation.3.clone | custom fusion | bytes 73728 | tf_op jit(solution)/shard_map/jit(_take)/gather | solution.py:96
  527.7 4.6 fusion.16
  540.3 24.2 %reduce-scatter.4.cloned.1.call-done = f32[256,4]{1,0:T(8,128)} async-done(((f32[1024,4]{1,0:T(8,128)}), f32[256,4]{1,0:T(8,128)}) %reduce-scatter.4.cloned.1.call-update) | async-done | bytes 4112
  567.1 39.5 %psum.7 = f32[]{:T(128)} all-reduce(f32[]{:T(128)} %multiply_reduce_fusion), channel_id=1, replica_groups=mesh['span'=8,'plane'=4] {'span','plane'}, use_global_device_ids=true, to_apply=%region_5.8 | all-reduce | flops 1 | bytes 8 | tf_op jit(solution)/shard_map/psum | solution.py:136
  (203 shorter events, 127.5 us)
Async XLA Ops:
  7.2 7.3 %copy-start.13 = (f32[9,9,1,1,1]{1,0,4,3,2:T(8,128)S(1)}, f32[9,9,1,1,1]{1,0,4,3,2:T(8,128)}, u32[]{:S(2)}) copy-start(f32[9,9,1,1,1]{1,0,4,3,2:T(8,128)} %constant.82) | copy-start | bytes 976
  7.2 7.3 %copy-start = (f32[3,4,81,128]{3,1,2,0:T(4,128)S(1)}, f32[3,4,81,128]{3,1,2,0:T(4,128)}, u32[]{:S(2)}) copy-start(f32[3,4,81,128]{3,1,2,0:T(4,128)} %param.21) | copy-start | bytes 1492996
  19.2 14.4 %copy-start.14 = (f32[4,81,81]{2,0,1:T(4,128)S(1)}, f32[4,81,81]{2,0,1:T(4,128)}, u32[]{:S(2)}) copy-start(f32[4,81,81]{2,0,1:T(4,128)} %param.25) | copy-start | bytes 314932
  22.9 146.0 %collective-permute-start.6 = (f32[3,4,81,16]{3,1,2,0:T(4,128)S(1)}, f32[3,4,81,16]{3,1,2,0:T(4,128)}, u32[]{:S(2)}, u32[]{:S(2)}) collective-permute-start(f32[3,4,81,16]{3,1,2,0:T(4,128)S(1)} %get-tuple-element.32), channel_id=1, source_target_pairs={{0,28},{4,24},{8,20},{12,16},{16,12},{20,8},{24,4},{28,0},{1,29},{... | collective-permute-start | bytes 186632 | tf_op jit(solution)/shard_map/ppermute | solution.py:24
  28.9 138.7 %collective-permute-start.5 = (f32[3,4,81,16]{3,1,2,0:T(4,128)}, f32[3,4,81,16]{3,1,2,0:T(4,128)}, u32[]{:S(2)}, u32[]{:S(2)}) collective-permute-start(f32[3,4,81,16]{3,1,2,0:T(4,128)} %get-tuple-element.33), channel_id=1, source_target_pairs={{0,24},{4,28},{8,16},{12,20},{16,8},{20,12},{24,0},{28,4},{1,25},{... | collective-permute-start | bytes 186632 | tf_op jit(solution)/shard_map/ppermute | solution.py:24
  29.1 137.2 %collective-permute-start.4 = (f32[3,4,81,16]{3,1,2,0:T(4,128)}, f32[3,4,81,16]{3,1,2,0:T(4,128)}, u32[]{:S(2)}, u32[]{:S(2)}) collective-permute-start(f32[3,4,81,16]{3,1,2,0:T(4,128)} %get-tuple-element.34), channel_id=1, source_target_pairs={{0,20},{4,16},{8,28},{12,24},{16,4},{20,0},{24,12},{28,8},{1,21},{... | collective-permute-start | bytes 186632 | tf_op jit(solution)/shard_map/ppermute | solution.py:24
  29.9 135.2 %collective-permute-start.3 = (f32[3,4,81,16]{3,1,2,0:T(4,128)}, f32[3,4,81,16]{3,1,2,0:T(4,128)}, u32[]{:S(2)}, u32[]{:S(2)}) collective-permute-start(f32[3,4,81,16]{3,1,2,0:T(4,128)} %get-tuple-element.35), channel_id=1, source_target_pairs={{0,16},{4,20},{8,24},{12,28},{16,0},{20,4},{24,8},{28,12},{1,17},{... | collective-permute-start | bytes 186632 | tf_op jit(solution)/shard_map/ppermute | solution.py:24
  31.9 109.5 %collective-permute-start = (f32[3,4,81,16]{3,1,2,0:T(4,128)}, f32[3,4,81,16]{3,1,2,0:T(4,128)}, u32[]{:S(2)}, u32[]{:S(2)}) collective-permute-start(f32[3,4,81,16]{3,1,2,0:T(4,128)} %get-tuple-element.38), channel_id=1, source_target_pairs={{0,4},{4,0},{8,12},{12,8},{16,20},{20,16},{24,28},{28,24},{1,5},{5... | collective-permute-start | bytes 186632 | tf_op jit(solution)/shard_map/ppermute | solution.py:24
  141.4 12.2 %collective-permute-start.1 = (f32[3,4,81,16]{3,1,2,0:T(4,128)}, f32[3,4,81,16]{3,1,2,0:T(4,128)}, u32[]{:S(2)}, u32[]{:S(2)}) collective-permute-start(f32[3,4,81,16]{3,1,2,0:T(4,128)} %get-tuple-element.37), channel_id=1, source_target_pairs={{0,8},{4,12},{8,0},{12,4},{16,24},{20,28},{24,16},{28,20},{1,9},{5... | collective-permute-start | bytes 186632 | tf_op jit(solution)/shard_map/ppermute | solution.py:24
  153.6 10.1 %collective-permute-start.2 = (f32[3,4,81,16]{3,1,2,0:T(4,128)}, f32[3,4,81,16]{3,1,2,0:T(4,128)}, u32[]{:S(2)}, u32[]{:S(2)}) collective-permute-start(f32[3,4,81,16]{3,1,2,0:T(4,128)} %get-tuple-element.36), channel_id=1, source_target_pairs={{0,12},{4,8},{8,4},{12,0},{16,28},{20,24},{24,20},{28,16},{1,13},{... | collective-permute-start | bytes 186632 | tf_op jit(solution)/shard_map/ppermute | solution.py:24
  165.0 5.2 copy-start.10
  176.1 16.7 %all-to-all-start = ((f32[3,32,81,16]{2,3,0,1:T(8,128)}), f32[3,32,81,16]{2,3,0,1:T(8,128)S(1)}, u32[]{:S(2)}, u32[]{:S(2)}) async-start(f32[3,32,81,16]{2,3,0,1:T(8,128)} %copy.79), calls=%async_computation | async-start | bytes 1572864 | tf_op jit(solution)/shard_map/all_to_all | solution.py:91
  211.6 87.4 %collective-permute-start.13 = (f32[3,4,81,16]{3,1,2,0:T(4,128)S(1)}, f32[3,4,81,16]{3,1,2,0:T(4,128)}, u32[]{:S(2)}, u32[]{:S(2)}) collective-permute-start(f32[3,4,81,16]{3,1,2,0:T(4,128)S(1)} %get-tuple-element.24), channel_id=1, source_target_pairs={{0,28},{4,24},{8,20},{12,16},{16,12},{20,8},{24,4},{28,0},{1,29},{... | collective-permute-start | bytes 186632 | tf_op jit(solution)/shard_map/ppermute | solution.py:24
  213.9 83.8 %collective-permute-start.12 = (f32[3,4,81,16]{3,1,2,0:T(4,128)}, f32[3,4,81,16]{3,1,2,0:T(4,128)}, u32[]{:S(2)}, u32[]{:S(2)}) collective-permute-start(f32[3,4,81,16]{3,1,2,0:T(4,128)} %get-tuple-element.25), channel_id=1, source_target_pairs={{0,24},{4,28},{8,16},{12,20},{16,8},{20,12},{24,0},{28,4},{1,25},{... | collective-permute-start | bytes 186632 | tf_op jit(solution)/shard_map/ppermute | solution.py:24
  216.2 80.2 %collective-permute-start.11 = (f32[3,4,81,16]{3,1,2,0:T(4,128)}, f32[3,4,81,16]{3,1,2,0:T(4,128)}, u32[]{:S(2)}, u32[]{:S(2)}) collective-permute-start(f32[3,4,81,16]{3,1,2,0:T(4,128)} %get-tuple-element.26), channel_id=1, source_target_pairs={{0,20},{4,16},{8,28},{12,24},{16,4},{20,0},{24,12},{28,8},{1,21},{... | collective-permute-start | bytes 186632 | tf_op jit(solution)/shard_map/ppermute | solution.py:24
  216.2 78.9 %collective-permute-start.10 = (f32[3,4,81,16]{3,1,2,0:T(4,128)}, f32[3,4,81,16]{3,1,2,0:T(4,128)}, u32[]{:S(2)}, u32[]{:S(2)}) collective-permute-start(f32[3,4,81,16]{3,1,2,0:T(4,128)} %get-tuple-element.27), channel_id=1, source_target_pairs={{0,16},{4,20},{8,24},{12,28},{16,0},{20,4},{24,8},{28,12},{1,17},{... | collective-permute-start | bytes 186632 | tf_op jit(solution)/shard_map/ppermute | solution.py:24
  219.3 12.0 %collective-permute-start.7 = (f32[3,4,81,16]{3,1,2,0:T(4,128)}, f32[3,4,81,16]{3,1,2,0:T(4,128)}, u32[]{:S(2)}, u32[]{:S(2)}) collective-permute-start(f32[3,4,81,16]{3,1,2,0:T(4,128)} %get-tuple-element.30), channel_id=1, source_target_pairs={{0,4},{4,0},{8,12},{12,8},{16,20},{20,16},{24,28},{28,24},{1,5},{5... | collective-permute-start | bytes 186632 | tf_op jit(solution)/shard_map/ppermute | solution.py:24
  231.3 32.3 %collective-permute-start.8 = (f32[3,4,81,16]{3,1,2,0:T(4,128)}, f32[3,4,81,16]{3,1,2,0:T(4,128)}, u32[]{:S(2)}, u32[]{:S(2)}) collective-permute-start(f32[3,4,81,16]{3,1,2,0:T(4,128)} %get-tuple-element.29), channel_id=1, source_target_pairs={{0,8},{4,12},{8,0},{12,4},{16,24},{20,28},{24,16},{28,20},{1,9},{5... | collective-permute-start | bytes 186632 | tf_op jit(solution)/shard_map/ppermute | solution.py:24
  263.6 30.2 %collective-permute-start.9 = (f32[3,4,81,16]{3,1,2,0:T(4,128)}, f32[3,4,81,16]{3,1,2,0:T(4,128)}, u32[]{:S(2)}, u32[]{:S(2)}) collective-permute-start(f32[3,4,81,16]{3,1,2,0:T(4,128)} %get-tuple-element.28), channel_id=1, source_target_pairs={{0,12},{4,8},{8,4},{12,0},{16,28},{20,24},{24,20},{28,16},{1,13},{... | collective-permute-start | bytes 186632 | tf_op jit(solution)/shard_map/ppermute | solution.py:24
  295.1 5.2 copy-start.11
  306.1 17.7 %all-to-all-start.1 = ((f32[3,32,81,16]{2,3,0,1:T(8,128)}), f32[3,32,81,16]{2,3,0,1:T(8,128)S(1)}, u32[]{:S(2)}, u32[]{:S(2)}) async-start(f32[3,32,81,16]{2,3,0,1:T(8,128)} %copy.98), calls=%async_computation.1 | async-start | bytes 1572864 | tf_op jit(solution)/shard_map/all_to_all | solution.py:91
  342.2 88.5 %collective-permute-start.20 = (f32[3,4,81,16]{3,1,2,0:T(4,128)S(1)}, f32[3,4,81,16]{3,1,2,0:T(4,128)}, u32[]{:S(2)}, u32[]{:S(2)}) collective-permute-start(f32[3,4,81,16]{3,1,2,0:T(4,128)S(1)} %get-tuple-element.16), channel_id=1, source_target_pairs={{0,28},{4,24},{8,20},{12,16},{16,12},{20,8},{24,4},{28,0},{1,29},{... | collective-permute-start | bytes 186632 | tf_op jit(solution)/shard_map/ppermute | solution.py:24
  344.4 85.0 %collective-permute-start.19 = (f32[3,4,81,16]{3,1,2,0:T(4,128)S(1)}, f32[3,4,81,16]{3,1,2,0:T(4,128)}, u32[]{:S(2)}, u32[]{:S(2)}) collective-permute-start(f32[3,4,81,16]{3,1,2,0:T(4,128)S(1)} %get-tuple-element.17), channel_id=1, source_target_pairs={{0,24},{4,28},{8,16},{12,20},{16,8},{20,12},{24,0},{28,4},{1,25},{... | collective-permute-start | bytes 186632 | tf_op jit(solution)/shard_map/ppermute | solution.py:24
  346.7 81.4 %collective-permute-start.18 = (f32[3,4,81,16]{3,1,2,0:T(4,128)}, f32[3,4,81,16]{3,1,2,0:T(4,128)}, u32[]{:S(2)}, u32[]{:S(2)}) collective-permute-start(f32[3,4,81,16]{3,1,2,0:T(4,128)} %get-tuple-element.18), channel_id=1, source_target_pairs={{0,20},{4,16},{8,28},{12,24},{16,4},{20,0},{24,12},{28,8},{1,21},{... | collective-permute-start | bytes 186632 | tf_op jit(solution)/shard_map/ppermute | solution.py:24
  346.7 80.1 %collective-permute-start.17 = (f32[3,4,81,16]{3,1,2,0:T(4,128)}, f32[3,4,81,16]{3,1,2,0:T(4,128)}, u32[]{:S(2)}, u32[]{:S(2)}) collective-permute-start(f32[3,4,81,16]{3,1,2,0:T(4,128)} %get-tuple-element.19), channel_id=1, source_target_pairs={{0,16},{4,20},{8,24},{12,28},{16,0},{20,4},{24,8},{28,12},{1,17},{... | collective-permute-start | bytes 186632 | tf_op jit(solution)/shard_map/ppermute | solution.py:24
  349.9 12.0 %collective-permute-start.14 = (f32[3,4,81,16]{3,1,2,0:T(4,128)}, f32[3,4,81,16]{3,1,2,0:T(4,128)}, u32[]{:S(2)}, u32[]{:S(2)}) collective-permute-start(f32[3,4,81,16]{3,1,2,0:T(4,128)} %get-tuple-element.22), channel_id=1, source_target_pairs={{0,4},{4,0},{8,12},{12,8},{16,20},{20,16},{24,28},{28,24},{1,5},{5... | collective-permute-start | bytes 186632 | tf_op jit(solution)/shard_map/ppermute | solution.py:24
  361.9 31.8 %collective-permute-start.15 = (f32[3,4,81,16]{3,1,2,0:T(4,128)}, f32[3,4,81,16]{3,1,2,0:T(4,128)}, u32[]{:S(2)}, u32[]{:S(2)}) collective-permute-start(f32[3,4,81,16]{3,1,2,0:T(4,128)} %get-tuple-element.21), channel_id=1, source_target_pairs={{0,8},{4,12},{8,0},{12,4},{16,24},{20,28},{24,16},{28,20},{1,9},{5... | collective-permute-start | bytes 186632 | tf_op jit(solution)/shard_map/ppermute | solution.py:24
  393.7 31.9 %collective-permute-start.16 = (f32[3,4,81,16]{3,1,2,0:T(4,128)}, f32[3,4,81,16]{3,1,2,0:T(4,128)}, u32[]{:S(2)}, u32[]{:S(2)}) collective-permute-start(f32[3,4,81,16]{3,1,2,0:T(4,128)} %get-tuple-element.20), channel_id=1, source_target_pairs={{0,12},{4,8},{8,4},{12,0},{16,28},{20,24},{24,20},{28,16},{1,13},{... | collective-permute-start | bytes 186632 | tf_op jit(solution)/shard_map/ppermute | solution.py:24
  426.8 5.2 copy-start.12
  436.5 5.6 copy-start.17
  437.9 74.0 %all-to-all-start.2 = ((f32[3,32,81,16]{2,3,0,1:T(8,128)}), f32[3,32,81,16]{2,3,0,1:T(8,128)S(1)}, u32[]{:S(2)}, u32[]{:S(2)}) async-start(f32[3,32,81,16]{2,3,0,1:T(8,128)} %copy.117), calls=%async_computation.2 | async-start | bytes 1572864 | tf_op jit(solution)/shard_map/all_to_all | solution.py:91
  441.4 123.0 %reduce-scatter.4.cloned.1.call-start = ((), (), s32[]{:S(2)}) async-start(), calls=%async_computation.4 | async-start | bytes 655360
  (18 other events, 37.1 us)
Sparse Core Ops, SparseCore 0:
  540.4 24.0 reduce-scatter.3
